TPU v7x, 256 devices: a whole 4x4x8 slice. The times are simulated.
256 devices in a mesh: section: 2 (over core), row: 32 (over z, y), col: 4 (over x).
Axes of the slice: x: 4, y: 4, z: 8, core: 2. Of those that a mesh axis runs over, the one named last changes fastest.
Arguments:
- hidden_in: bfloat16 [32, 256, 3072], P('row', None, 'col')
- patch_ends: int32 [32, 4], P('row'), may hold values from 1 to 256, as said below
- timestep: int32 [32], P('row'), may hold values from 0 to 999
- mod_weight: bfloat16 [2, 256, 3, 3072], P('section'), may hold values from -0.75 to 0.75
- qkv_weight: bfloat16 [2, 3072, 3, 3072], P('section', 'row', None, 'col'), may hold values from -0.109375 to 0.109375
- out_weight: bfloat16 [2, 3072, 3072], P('section', 'col', 'row'), may hold values from -0.109375 to 0.109375
- stale_keys: bfloat16 [2, 32, 256, 3072], P('section', 'row', None, 'col'), may hold values from -1.5 to 1.5
- stale_values: bfloat16 [2, 32, 256, 3072], P('section', 'row', None, 'col'), may hold values from -6 to 6
Outputs:
- layer_out: bfloat16 [2, 32, 256, 3072], P('section', 'row', None, 'col')
Inputs may be any that keep to these rules, and one draw needn't show every extreme that they name: patch_ends rises along each request's 4 patches; each patch holds at least one and at most 64 positions, and in every draw some request has all 4 patches of exactly 64 positions.
All inputs are finite; a program needn't handle non-finite values.
Results may differ from a plain program's by a relative error of at most 0.018.
Values may be sent and summed in bfloat16 or wider, within the bound.
A program may use at most 128 MiB of HBM per device.

v0:
```python
import math
import jax
import jax.numpy as jnp
from jax import lax
from jax.sharding import PartitionSpec as P

HD = 128
FREQ = 256
NP = 4
PATCH = 64


def passed_along(array, axis, by):
    length = lax.axis_size(axis)
    pairs = [(i, i + by) for i in range(length) if 0 <= i + by < length]
    return lax.ppermute(array, axis, pairs)


def embed_time(timestep, feat_width):
    half_width = feat_width // 2
    frequency = jnp.exp(
        jnp.arange(half_width, dtype=jnp.float32) * (-math.log(10000.0) / half_width)
    )
    angles = timestep.astype(jnp.float32)[:, None] * frequency[None, :]
    return jnp.concatenate([jnp.cos(angles), jnp.sin(angles)], axis=1).astype(jnp.bfloat16)


def head_norm(raw_proj):
    shaped = raw_proj.reshape(raw_proj.shape[:-1] + (raw_proj.shape[-1] // HD, HD))
    scaled = shaped / jnp.sqrt(jnp.mean(shaped * shaped, axis=-1, keepdims=True) + 1e-06)
    return scaled.reshape(raw_proj.shape).astype(jnp.bfloat16)


def slice_one(source, first_row):
    return lax.dynamic_slice_in_dim(source, first_row, PATCH, 0)


def update_one(source, new_rows, first_row):
    return lax.dynamic_update_slice_in_dim(source, new_rows, first_row, 0)


def take_rows(source, row_begin):
    return jax.vmap(slice_one)(source, row_begin)


def put_rows(source, new_rows, row_begin, row_count, is_active):
    previous = take_rows(source, row_begin)
    keep_new = (jnp.arange(PATCH)[None, :, None] < row_count[:, None, None]) & is_active
    merged = jnp.where(keep_new, new_rows, previous)
    return jax.vmap(update_one)(source, merged, row_begin)


def attend_rows(queries, key_rows, value_rows, key_ok):
    requests = queries.shape[0]
    query_heads = queries.reshape(requests, queries.shape[1], -1, HD)
    key_heads = key_rows.reshape(requests, key_rows.shape[1], -1, HD)
    value_heads = value_rows.reshape(requests, value_rows.shape[1], -1, HD)
    scores = jnp.einsum(
        "bqhd,bkhd->bhqk", query_heads, key_heads, preferred_element_type=jnp.float32
    ) / math.sqrt(HD)
    weights = jnp.exp(scores) * key_ok[:, None, None, :]
    weights = (weights / jnp.sum(weights, axis=-1, keepdims=True)).astype(jnp.bfloat16)
    mixed = jnp.einsum("bhqk,bkhd->bqhd", weights, value_heads, preferred_element_type=jnp.float32)
    return mixed.reshape(queries.shape).astype(jnp.bfloat16)


def modulated_rows(patch_rows, shift_vec, scale_vec, col_index, col_width):
    feat_width = shift_vec.shape[-1]
    as_float = patch_rows.astype(jnp.float32)
    sum_rows, sum_squares = lax.psum(
        (jnp.sum(as_float, axis=-1), jnp.sum(as_float * as_float, axis=-1)), "col"
    )
    row_mean = (sum_rows / feat_width)[:, :, None]
    row_var = (sum_squares / feat_width)[:, :, None] - row_mean * row_mean
    shift_own = lax.dynamic_slice_in_dim(shift_vec, col_index * col_width, col_width, 1)
    scale_own = lax.dynamic_slice_in_dim(scale_vec, col_index * col_width, col_width, 1)
    normed = (as_float - row_mean) / jnp.sqrt(row_var + 1e-06)
    local_rows = (normed * (1.0 + scale_own[:, None, :]) + shift_own[:, None, :]).astype(
        jnp.bfloat16
    )
    return lax.all_gather(local_rows, "col", axis=2, tiled=True)


def shards(
    hidden_in, patch_ends, timestep, mod_weight, qkv_weight, out_weight, stale_keys, stale_values
):
    section_index = lax.axis_index("section")
    col_index = lax.axis_index("col")
    requests, slot_len, col_width = hidden_in.shape
    feat_width = mod_weight.shape[-1]
    qkv_full = lax.all_gather(qkv_weight, "row", axis=1, tiled=True)
    out_full = lax.all_gather(out_weight, "row", axis=2, tiled=True)
    qkv_matrix = qkv_full[0].reshape(feat_width, 3 * col_width)
    out_matrix = out_full[0]
    time_feats = embed_time(timestep, FREQ)
    modulation = jnp.dot(
        time_feats, mod_weight[0].reshape(FREQ, 3 * feat_width), preferred_element_type=jnp.float32
    ).reshape(requests, 3, feat_width)
    shift_vec = modulation[:, 0]
    scale_vec = modulation[:, 1]
    gate_own = lax.dynamic_slice_in_dim(modulation[:, 2], col_index * col_width, col_width, 1)
    padding = jnp.zeros((requests, PATCH, col_width), jnp.bfloat16)
    input_pad = jnp.concatenate([hidden_in, padding], axis=1)
    key_cache = jnp.concatenate([stale_keys[0], padding], axis=1)
    value_cache = jnp.concatenate([stale_values[0], padding], axis=1)
    result_pad = jnp.zeros((requests, slot_len + PATCH, col_width), jnp.bfloat16)
    patch_starts = jnp.concatenate(
        [jnp.zeros((requests, 1), jnp.int32), patch_ends[:, : NP - 1]], axis=1
    )
    seq_len = patch_ends[:, NP - 1]
    key_ok = (jnp.arange(slot_len)[None, :] < seq_len[:, None]).astype(jnp.float32)
    row_ids = jnp.arange(PATCH)
    received = padding
    for step_index in range(NP + 1):
        offset = step_index - section_index
        is_active = (offset >= 0) & (offset < NP)
        patch_index = jnp.clip(offset, 0, NP - 1)
        row_begin = jnp.take(patch_starts, patch_index, axis=1)
        row_count = jnp.take(patch_ends, patch_index, axis=1) - row_begin
        patch_rows = jnp.where(section_index == 0, take_rows(input_pad, row_begin), received)
        modulated = modulated_rows(patch_rows, shift_vec, scale_vec, col_index, col_width)
        projected = jnp.dot(
            modulated.reshape(-1, feat_width), qkv_matrix, preferred_element_type=jnp.float32
        ).reshape(requests, PATCH, 3, col_width)
        queries = head_norm(projected[:, :, 0])
        key_cache = put_rows(
            key_cache, head_norm(projected[:, :, 1]), row_begin, row_count, is_active
        )
        value_cache = put_rows(
            value_cache, projected[:, :, 2].astype(jnp.bfloat16), row_begin, row_count, is_active
        )
        attended = attend_rows(queries, key_cache[:, :slot_len], value_cache[:, :slot_len], key_ok)
        partial_out = jnp.dot(
            attended.reshape(-1, col_width), out_matrix, preferred_element_type=jnp.float32
        ).reshape(requests, PATCH, feat_width)
        summed = lax.psum_scatter(
            partial_out.astype(jnp.bfloat16), "col", scatter_dimension=2, tiled=True
        ).astype(jnp.float32)
        updated = patch_rows.astype(jnp.float32) + gate_own[:, None, :] * summed
        within = row_ids[None, :, None] < row_count[:, None, None]
        new_rows = jnp.where(within, updated, 0.0).astype(jnp.bfloat16)
        result_pad = put_rows(result_pad, new_rows, row_begin, row_count, is_active)
        if step_index < NP:
            received = passed_along(new_rows, "section", 1)
    return result_pad[None, :, :slot_len]


def solution(mesh):
    return jax.shard_map(
        shards,
        mesh=mesh,
        in_specs=(
            P("row", None, "col"),
            P("row", None),
            P("row"),
            P("section", None, None, None),
            P("section", "row", None, "col"),
            P("section", "col", "row"),
            P("section", "row", None, "col"),
            P("section", "row", None, "col"),
        ),
        out_specs=P("section", "row", None, "col"),
        check_vma=False,
    )
```

profile of v0, /device:TPU:8, one launch (start us, length us, event | category | flops | bytes accessed | tf_op | source)
XLA Modules:
  0.0 542.1 jit_solution(13146894626585429524)
XLA Ops:
  8.8 1.6 constant_dynamic-slice_fusion.8
  17.1 6.7 %copy.135 = bf16[1,256,3,3072]{1,3,2,0:T(8,128)(2,1)} copy(bf16[1,256,3,3072]{3,1,2,0:T(8,128)(2,1)} %param.41) | data formatting | bytes 9437184 | tf_op args[3]
  23.9 10.5 %all-reduce.7 = (f32[1,64]{1,0:T(1,128)S(1)}, f32[1,64]{1,0:T(1,128)S(1)}) all-reduce(f32[1,64]{1,0:T(1,128)S(1)} %bitcast.463, f32[1,64]{1,0:T(1,128)S(1)} %bitcast.462), channel_id=1, replica_groups=mesh['section'=2,'row'=32,'col'=4] {'col'}, use_global_device_ids=true, to_apply=%region_4.5 | all-reduce | flops 128 | bytes 1024 | tf_op jit(solution)/shard_map/psum | solution.py:70
  34.4 3.7 fusion.10
  40.9 4.6 and_reduce_fusion
  45.6 12.5 %all_gather.21 = bf16[1,64,3072]{2,1,0:T(8,128)(2,1)S(1)} all-gather(bf16[1,64,768]{2,1,0:T(8,128)(2,1)S(1)} %fusion.90), channel_id=1, replica_groups=mesh['section'=2,'row'=32,'col'=4] {'col'}, dimensions={2}, use_global_device_ids=true | all-gather | bytes 491520 | tf_op jit(solution)/shard_map/all_gather | solution.py:81
  58.1 81.0 %all-gather.3.cloned.1.call-done = bf16[1,3072,3,768]{3,1,2,0:T(8,128)(2,1)} async-done(((bf16[1,96,3,768]{3,1,2,0:T(8,128)(2,1)}), bf16[1,3072,3,768]{3,1,2,0:T(8,128)(2,1)}) %all-gather.3.cloned.1.call-update) | async-done | bytes 14155792 | tf_op jit(solution)/shard_map/all_gather | solution.py:91
  139.1 18.7 %copy.136 = bf16[1,3072,3,768]{1,3,2,0:T(8,128)(2,1)} copy(bf16[1,3072,3,768]{3,1,2,0:T(8,128)(2,1)} %all-gather.3.cloned.1.call-done) | data formatting | bytes 28311552 | tf_op jit(solution)/shard_map/all_gather | solution.py:91
  157.8 9.5 %fusion.52 = f32[1,64,3,768]{3,1,2,0:T(8,128)S(1)} fusion(bf16[1,3072,3,768]{1,3,2,0:T(8,128)(2,1)} %copy.136, bf16[1,64,3072]{2,1,0:T(8,128)(2,1)S(1)} %all_gather.21), kind=kOutput, calls=%fused_computation.32 | convolution fusion | flops 905969664 | bytes 15138816 | tf_op jit(solution)/shard_map/dot_general | solution.py:122
  175.3 47.0 %all-gather.5.cloned.1.call-done = bf16[1,768,3072]{1,2,0:T(8,128)(2,1)} async-done(((bf16[1,768,96]{1,2,0:T(8,128)(2,1)}), bf16[1,768,3072]{1,2,0:T(8,128)(2,1)}) %all-gather.5.cloned.1.call-update) | async-done | bytes 4718608 | tf_op jit(solution)/shard_map/all_gather | solution.py:92
  222.4 4.6 fusion.49
  229.0 3.3 and_reduce_fusion.2
  232.3 16.8 %reduce-scatter.6.cloned.1.call-done = bf16[1,64,768]{2,1,0:T(8,128)(2,1)} async-done(((bf16[1,64,3072]{2,1,0:T(8,128)(2,1)}), bf16[1,64,768]{2,1,0:T(8,128)(2,1)}) %reduce-scatter.6.cloned.1.call-update) | async-done | bytes 98320 | tf_op jit(solution)/shard_map/reduce_scatter | solution.py:136
  249.0 1.6 select_select_fusion
  253.0 8.6 %all-reduce.6 = (f32[1,64]{1,0:T(1,128)S(1)}, f32[1,64]{1,0:T(1,128)S(1)}) all-reduce(f32[1,64]{1,0:T(1,128)S(1)} %bitcast.457, f32[1,64]{1,0:T(1,128)S(1)} %bitcast.456), channel_id=1, replica_groups=mesh['section'=2,'row'=32,'col'=4] {'col'}, use_global_device_ids=true, to_apply=%region_13.14 | all-reduce | flops 128 | bytes 1024 | tf_op jit(solution)/shard_map/psum | solution.py:70
  261.8 12.9 %all_gather.24 = bf16[1,64,3072]{2,1,0:T(8,128)(2,1)S(1)} all-gather(bf16[1,64,768]{2,1,0:T(8,128)(2,1)S(1)} %fusion.97), channel_id=1, replica_groups=mesh['section'=2,'row'=32,'col'=4] {'col'}, dimensions={2}, use_global_device_ids=true | all-gather | bytes 491520 | tf_op jit(solution)/shard_map/all_gather | solution.py:81
  274.6 9.4 %fusion.55 = f32[1,64,3,768]{3,1,2,0:T(8,128)S(1)} fusion(bf16[1,3072,3,768]{1,3,2,0:T(8,128)(2,1)} %copy.136, bf16[1,64,3072]{2,1,0:T(8,128)(2,1)S(1)} %all_gather.24), kind=kOutput, calls=%fused_computation.33 | convolution fusion | flops 905969664 | bytes 15138816 | tf_op jit(solution)/shard_map/dot_general | solution.py:122
  290.7 4.6 fusion.46
  297.4 21.2 %reduce-scatter.8.cloned.1.call-done = bf16[1,64,768]{2,1,0:T(8,128)(2,1)} async-done(((bf16[1,64,3072]{2,1,0:T(8,128)(2,1)}), bf16[1,64,768]{2,1,0:T(8,128)(2,1)}) %reduce-scatter.8.cloned.1.call-update) | async-done | bytes 98320 | tf_op jit(solution)/shard_map/reduce_scatter | solution.py:136
  318.7 2.3 fusion.186
  323.4 8.6 %all-reduce.5 = (f32[1,64]{1,0:T(1,128)S(1)}, f32[1,64]{1,0:T(1,128)S(1)}) all-reduce(f32[1,64]{1,0:T(1,128)S(1)} %bitcast.459, f32[1,64]{1,0:T(1,128)S(1)} %bitcast.458), channel_id=1, replica_groups=mesh['section'=2,'row'=32,'col'=4] {'col'}, use_global_device_ids=true, to_apply=%region_22.23 | all-reduce | flops 128 | bytes 1024 | tf_op jit(solution)/shard_map/psum | solution.py:70
  332.1 12.7 %all_gather.25 = bf16[1,64,3072]{2,1,0:T(8,128)(2,1)S(1)} all-gather(bf16[1,64,768]{2,1,0:T(8,128)(2,1)S(1)} %fusion.104), channel_id=1, replica_groups=mesh['section'=2,'row'=32,'col'=4] {'col'}, dimensions={2}, use_global_device_ids=true | all-gather | bytes 491520 | tf_op jit(solution)/shard_map/all_gather | solution.py:81
  344.8 9.4 %fusion.58 = f32[1,64,3,768]{3,1,2,0:T(8,128)S(1)} fusion(bf16[1,3072,3,768]{1,3,2,0:T(8,128)(2,1)} %copy.136, bf16[1,64,3072]{2,1,0:T(8,128)(2,1)S(1)} %all_gather.25), kind=kOutput, calls=%fused_computation.34 | convolution fusion | flops 905969664 | bytes 15138816 | tf_op jit(solution)/shard_map/dot_general | solution.py:122
  355.2 2.0 fusion.142
  361.4 4.6 fusion.43
  368.2 21.1 %reduce-scatter.10.cloned.1.call-done = bf16[1,64,768]{2,1,0:T(8,128)(2,1)} async-done(((bf16[1,64,3072]{2,1,0:T(8,128)(2,1)}), bf16[1,64,768]{2,1,0:T(8,128)(2,1)}) %reduce-scatter.10.cloned.1.call-update) | async-done | bytes 98320 | tf_op jit(solution)/shard_map/reduce_scatter | solution.py:136
  389.3 2.3 fusion.185
  391.6 1.5 collective-permute-start.2
  394.0 8.6 %all-reduce.4 = (f32[1,64]{1,0:T(1,128)S(1)}, f32[1,64]{1,0:T(1,128)S(1)}) all-reduce(f32[1,64]{1,0:T(1,128)S(1)} %bitcast.461, f32[1,64]{1,0:T(1,128)S(1)} %bitcast.460), channel_id=1, replica_groups=mesh['section'=2,'row'=32,'col'=4] {'col'}, use_global_device_ids=true, to_apply=%region_31.32 | all-reduce | flops 128 | bytes 1024 | tf_op jit(solution)/shard_map/psum | solution.py:70
  402.8 12.6 %all_gather.26 = bf16[1,64,3072]{2,1,0:T(8,128)(2,1)S(1)} all-gather(bf16[1,64,768]{2,1,0:T(8,128)(2,1)S(1)} %fusion.111), channel_id=1, replica_groups=mesh['section'=2,'row'=32,'col'=4] {'col'}, dimensions={2}, use_global_device_ids=true | all-gather | bytes 491520 | tf_op jit(solution)/shard_map/all_gather | solution.py:81
  415.4 9.4 %fusion.61 = f32[1,64,3,768]{3,1,2,0:T(8,128)S(1)} fusion(bf16[1,3072,3,768]{1,3,2,0:T(8,128)(2,1)} %copy.136, bf16[1,64,3072]{2,1,0:T(8,128)(2,1)S(1)} %all_gather.26), kind=kOutput, calls=%fused_computation.35 | convolution fusion | flops 905969664 | bytes 15138816 | tf_op jit(solution)/shard_map/dot_general | solution.py:122
  425.8 2.0 fusion.144
  427.8 1.5 scatter.66
  429.3 1.5 scatter.65
  432.0 4.6 fusion.40
  438.8 21.3 %reduce-scatter.12.cloned.1.call-done = bf16[1,64,768]{2,1,0:T(8,128)(2,1)} async-done(((bf16[1,64,3072]{2,1,0:T(8,128)(2,1)}), bf16[1,64,768]{2,1,0:T(8,128)(2,1)}) %reduce-scatter.12.cloned.1.call-update) | async-done | bytes 98320 | tf_op jit(solution)/shard_map/reduce_scatter | solution.py:136
  460.1 2.3 fusion.184
  464.7 8.6 %all-reduce.3 = (f32[1,64]{1,0:T(1,128)S(1)}, f32[1,64]{1,0:T(1,128)S(1)}) all-reduce(f32[1,64]{1,0:T(1,128)S(1)} %bitcast.455, f32[1,64]{1,0:T(1,128)S(1)} %bitcast.454), channel_id=1, replica_groups=mesh['section'=2,'row'=32,'col'=4] {'col'}, use_global_device_ids=true, to_apply=%region_40.41 | all-reduce | flops 128 | bytes 1024 | tf_op jit(solution)/shard_map/psum | solution.py:70
  473.4 13.0 %all_gather.27 = bf16[1,64,3072]{2,1,0:T(8,128)(2,1)S(1)} all-gather(bf16[1,64,768]{2,1,0:T(8,128)(2,1)S(1)} %fusion.118), channel_id=1, replica_groups=mesh['section'=2,'row'=32,'col'=4] {'col'}, dimensions={2}, use_global_device_ids=true | all-gather | bytes 491520 | tf_op jit(solution)/shard_map/all_gather | solution.py:81
  486.4 9.4 %fusion.64 = f32[1,64,3,768]{3,1,2,0:T(8,128)S(1)} fusion(bf16[1,3072,3,768]{1,3,2,0:T(8,128)(2,1)} %copy.136, bf16[1,64,3072]{2,1,0:T(8,128)(2,1)S(1)} %all_gather.27), kind=kOutput, calls=%fused_computation.36 | convolution fusion | flops 905969664 | bytes 15138816 | tf_op jit(solution)/shard_map/dot_general | solution.py:122
  496.8 1.5 fusion.146
  498.3 1.5 scatter.71
  500.1 1.5 scatter.70
  502.7 4.6 fusion.37
  507.3 1.5 scatter.69
  508.8 21.8 %reduce-scatter.14.cloned.1.call-done = bf16[1,64,768]{2,1,0:T(8,128)(2,1)} async-done(((bf16[1,64,3072]{2,1,0:T(8,128)(2,1)}), bf16[1,64,768]{2,1,0:T(8,128)(2,1)}) %reduce-scatter.14.cloned.1.call-update) | async-done | bytes 98320 | tf_op jit(solution)/shard_map/reduce_scatter | solution.py:136
  530.6 2.4 fusion.163
  533.0 1.5 scatter.74
  (206 shorter events, 46.4 us)
Async XLA Ops:
  6.5 132.6 %all-gather.3.cloned.1.call-start = ((), (), s32[]{:S(2)}) async-start(), calls=%async_computation.5 | async-start | bytes 14598144 | tf_op jit(solution)/shard_map/all_gather | solution.py:91
  7.3 215.1 %all-gather.5.cloned.1.call-start = ((), (), s32[]{:S(2)}) async-start(), calls=%async_computation.6 | async-start | bytes 4866048 | tf_op jit(solution)/shard_map/all_gather | solution.py:92
  8.0 241.0 %reduce-scatter.6.cloned.1.call-start = ((), (), s32[]{:S(2)}) async-start(), calls=%async_computation.7 | async-start | bytes 491520 | tf_op jit(solution)/shard_map/reduce_scatter | solution.py:136
  17.1 6.7 %copy-start = (bf16[1,256,768]{2,1,0:T(8,128)(2,1)S(1)}, bf16[1,256,768]{2,1,0:T(8,128)(2,1)}, u32[]{:S(2)}) copy-start(bf16[1,256,768]{2,1,0:T(8,128)(2,1)} %param.38) | copy-start | bytes 1179652
  23.8 15.1 %copy-start.3 = (s32[1,2]{1,0:T(1,128)S(1)}, s32[1,2]{1,0:T(1,128)}, u32[]{:S(2)}) copy-start(s32[1,2]{1,0:T(1,128)} %constant.478.clone.1) | copy-start | bytes 28
  23.8 17.1 %copy-start.4 = (s32[3]{0:T(128)S(1)}, s32[3]{0:T(128)}, u32[]{:S(2)}) copy-start(s32[3]{0:T(128)} %constant.479.clone.1) | copy-start | bytes 40
  157.8 12.2 %copy-start.1 = (bf16[1,1,256,768]{3,2,1,0:T(8,128)(2,1)S(1)}, bf16[1,1,256,768]{3,2,1,0:T(8,128)(2,1)}, u32[]{:S(2)}) copy-start(bf16[1,1,256,768]{3,2,1,0:T(8,128)(2,1)} %param.45) | copy-start | bytes 1179652
  157.8 12.2 %copy-start.2 = (bf16[1,1,256,768]{3,2,1,0:T(8,128)(2,1)S(1)}, bf16[1,1,256,768]{3,2,1,0:T(8,128)(2,1)}, u32[]{:S(2)}) copy-start(bf16[1,1,256,768]{3,2,1,0:T(8,128)(2,1)} %param.44) | copy-start | bytes 1179652
  227.0 91.6 %reduce-scatter.8.cloned.1.call-start = ((), (), s32[]{:S(2)}) async-start(), calls=%async_computation.8 | async-start | bytes 491520 | tf_op jit(solution)/shard_map/reduce_scatter | solution.py:136
  250.6 2.2 collective-permute-start
  295.3 94.0 %reduce-scatter.10.cloned.1.call-start = ((), (), s32[]{:S(2)}) async-start(), calls=%async_computation.9 | async-start | bytes 491520 | tf_op jit(solution)/shard_map/reduce_scatter | solution.py:136
  321.0 2.2 collective-permute-start.1
  360.8 28.5 %copy-start.6 = (pred[64]{0:T(512)(128)(4,1)S(1)}, pred[64]{0:T(512)(128)(4,1)}, u32[]{:S(2)}) copy-start(pred[64]{0:T(512)(128)(4,1)} %broadcast_and_fusion.2) | copy-start | bytes 196
  366.0 94.0 %reduce-scatter.12.cloned.1.call-start = ((), (), s32[]{:S(2)}) async-start(), calls=%async_computation.10 | async-start | bytes 491520 | tf_op jit(solution)/shard_map/reduce_scatter | solution.py:136
  391.6 2.2 collective-permute-start.2
  431.4 28.6 %copy-start.5 = (pred[64]{0:T(512)(128)(4,1)S(1)}, pred[64]{0:T(512)(128)(4,1)}, u32[]{:S(2)}) copy-start(pred[64]{0:T(512)(128)(4,1)} %broadcast_and_fusion.1) | copy-start | bytes 196
  436.7 93.9 %reduce-scatter.14.cloned.1.call-start = ((), (), s32[]{:S(2)}) async-start(), calls=%async_computation.11 | async-start | bytes 491520 | tf_op jit(solution)/shard_map/reduce_scatter | solution.py:136
  462.3 2.2 collective-permute-start.3
Sparse Core Ops, SparseCore 0:
  9.9 129.1 all-gather.2
  141.7 80.6 all-gather.4
  227.1 21.8 reduce-scatter.5
  295.5 23.1 reduce-scatter.7
  366.2 23.0 reduce-scatter.9
  436.8 23.2 reduce-scatter.11
  507.4 23.0 reduce-scatter.13
where the time goes:
time: 544 us; the launch traced here: 542 us
  waiting for transfers between devices  234 us (43%)
  blocking collectives  109 us (20%)
  matrix products  76.5 us (14%)
  local copies, waits for them, and re-layouts  61.6 us (11%)
  other arithmetic  34.5 us (6%)
  between operations  21.4 us (4%)
  starting transfers between devices  5.65 us (1%)
    reduce_scatter x5, waiting for transfers between devices, shards(): lax.psum_scatter(partial_out.astype(jnp.bfloat16), 'col', scatter_dimensi...  102 us
    all_gather x1, waiting for transfers between devices, shards(): qkv_full = lax.all_gather(qkv_weight, 'row', axis=1, tiled=True)  81 us
    all_gather x5, blocking collectives, modulated_rows(): return lax.all_gather(local_rows, 'col', axis=2, tiled=True)  63.6 us
    dot_general x5, matrix products, shards(): jnp.dot(modulated.reshape(-1, feat_width), qkv_matrix, preferred_element_...  47.1 us
    all_gather x1, waiting for transfers between devices, shards(): out_full = lax.all_gather(out_weight, 'row', axis=2, tiled=True)  47 us
    psum x5, blocking collectives, modulated_rows(): lax.psum((jnp.sum(as_float, axis=-1), jnp.sum(as_float * as_float, axis=-...  44.9 us
    another operation x13, other arithmetic  27.1 us
    dot_general x5, matrix products, shards(): jnp.dot(attended.reshape(-1, col_width), out_matrix, preferred_element_ty...  23.1 us
  transfers between devices with their start and end apart: 11, of which 11 were waited for; matrix products, arithmetic and copies ran while one was open for 13% of the time, Pallas kernels for 0%

commit v1 on v0

--- a/solution.py
+++ b/solution.py
@@ -3,6 +3,7 @@
 import jax.numpy as jnp
 from jax import lax
 from jax.sharding import PartitionSpec as P
+from jax.lax import all_to_all, axis_size
 
 HD = 128
 FREQ = 256
@@ -89,7 +90,9 @@
     requests, slot_len, col_width = hidden_in.shape
     feat_width = mod_weight.shape[-1]
     qkv_full = lax.all_gather(qkv_weight, "row", axis=1, tiled=True)
-    out_full = lax.all_gather(out_weight, "row", axis=2, tiled=True)
+    out_full = jnp.concatenate(
+        all_to_all(jnp.stack(axis_size("row") * [out_weight]), "row", 0, 0), 2
+    )
     qkv_matrix = qkv_full[0].reshape(feat_width, 3 * col_width)
     out_matrix = out_full[0]
     time_feats = embed_time(timestep, FREQ)

time: 544 us -> 568 us (1.044)
  waiting for transfers between devices: 234 us -> 247 us
  starting transfers between devices: 5.65 us -> 17.5 us
    all_gather x1, waiting for transfers between devices: 81 us -> 141 us  [shards(): qkv_full = lax.all_gather(qkv_weight, 'row', axis=1, tiled=True)]
    all_gather x1 -> x0, waiting for transfers between devices: 47 us -> none  [shards(): out_full = lax.all_gather(out_weight, 'row', axis=2, tiled=True)]
    all_to_all x0 -> x1, starting transfers between devices: none -> 11.9 us  [shards(): all_to_all(jnp.stack(axis_size('row') * [out_weight]), 'row', 0, 0)]
  transfers between devices with their start and end apart: 11 -> 11, of which waited for: 11 -> 10; matrix products, arithmetic and copies ran while one was open for 13% -> 12% of each run, Pallas kernels for 0% -> 0%
where the time goes in v1:
time: 568 us; the launch traced here: 566 us
  waiting for transfers between devices  247 us (43%)
  blocking collectives  109 us (19%)
  matrix products  76.3 us (13%)
  local copies, waits for them, and re-layouts  62.3 us (11%)
  other arithmetic  33.5 us (6%)
  between operations  21.7 us (4%)
  starting transfers between devices  17.5 us (3%)
    all_gather x1, waiting for transfers between devices, shards(): qkv_full = lax.all_gather(qkv_weight, 'row', axis=1, tiled=True)  141 us
    reduce_scatter x5, waiting for transfers between devices, shards(): lax.psum_scatter(partial_out.astype(jnp.bfloat16), 'col', scatter_dimensi...  102 us
    all_gather x5, blocking collectives, modulated_rows(): return lax.all_gather(local_rows, 'col', axis=2, tiled=True)  63.6 us
    dot_general x5, matrix products, shards(): jnp.dot(modulated.reshape(-1, feat_width), qkv_matrix, preferred_element_...  47 us
    psum x5, blocking collectives, modulated_rows(): lax.psum((jnp.sum(as_float, axis=-1), jnp.sum(as_float * as_float, axis=-...  44.9 us
    another operation x13, other arithmetic  26.8 us
    dot_general x5, matrix products, shards(): jnp.dot(attended.reshape(-1, col_width), out_matrix, preferred_element_ty...  23.1 us
    scatter x15, local copies, waits for them, and re-layouts, update_one(): return lax.dynamic_update_slice_in_dim(source, new_rows, first_row, 0)  22.2 us
  transfers between devices with their start and end apart: 11, of which 10 were waited for; matrix products, arithmetic and copies ran while one was open for 12% of the time, Pallas kernels for 0%

profile of v1, /device:TPU:8, one launch (start us, length us, event | category | flops | bytes accessed | tf_op | source)
XLA Modules:
  0.0 566.4 jit_solution(9769458300822851451)
XLA Ops:
  7.3 3.6 stack.2
  10.9 11.9 %all-to-all-start = ((bf16[32,1,768,96]{2,3,1,0:T(8,128)(2,1)}), bf16[32,1,768,96]{2,3,1,0:T(8,128)(2,1)}, u32[]{:S(2)}, u32[]{:S(2)}) async-start(bf16[32,1,768,96]{2,3,1,0:T(8,128)(2,1)} %stack.2), calls=%async_computation | async-start | bytes 9437184 | tf_op jit(solution)/shard_map/all_to_all | solution.py:94
  28.4 6.7 %copy.138 = bf16[1,256,3,3072]{1,3,2,0:T(8,128)(2,1)} copy(bf16[1,256,3,3072]{3,1,2,0:T(8,128)(2,1)} %param.41) | data formatting | bytes 9437184 | tf_op args[3]
  35.2 10.5 %all-reduce.7 = (f32[1,64]{1,0:T(1,128)S(1)}, f32[1,64]{1,0:T(1,128)S(1)}) all-reduce(f32[1,64]{1,0:T(1,128)S(1)} %bitcast.444, f32[1,64]{1,0:T(1,128)S(1)} %bitcast.443), channel_id=1, replica_groups=mesh['section'=2,'row'=32,'col'=4] {'col'}, use_global_device_ids=true, to_apply=%region_4.5 | all-reduce | flops 128 | bytes 1024 | tf_op jit(solution)/shard_map/psum | solution.py:71
  45.7 3.7 fusion.10
  52.1 4.5 and_reduce_fusion
  56.8 12.5 %all_gather.18 = bf16[1,64,3072]{2,1,0:T(8,128)(2,1)S(1)} all-gather(bf16[1,64,768]{2,1,0:T(8,128)(2,1)S(1)} %fusion.55), channel_id=1, replica_groups=mesh['section'=2,'row'=32,'col'=4] {'col'}, dimensions={2}, use_global_device_ids=true | all-gather | bytes 491520 | tf_op jit(solution)/shard_map/all_gather | solution.py:82
  69.3 141.3 %all-gather.2.cloned.1.call-done = bf16[1,3072,3,768]{3,1,2,0:T(8,128)(2,1)} async-done(((bf16[1,96,3,768]{3,1,2,0:T(8,128)(2,1)}), bf16[1,3072,3,768]{3,1,2,0:T(8,128)(2,1)}) %all-gather.2.cloned.1.call-update) | async-done | bytes 14155792 | tf_op jit(solution)/shard_map/all_gather | solution.py:92
  210.6 18.6 %copy.139 = bf16[1,3072,3,768]{1,3,2,0:T(8,128)(2,1)} copy(bf16[1,3072,3,768]{3,1,2,0:T(8,128)(2,1)} %all-gather.2.cloned.1.call-done) | data formatting | bytes 28311552 | tf_op jit(solution)/shard_map/all_gather | solution.py:92
  229.2 9.4 %fusion.17 = f32[1,64,3,768]{3,1,2,0:T(8,128)S(1)} fusion(bf16[1,3072,3,768]{1,3,2,0:T(8,128)(2,1)} %copy.139, bf16[1,64,3072]{2,1,0:T(8,128)(2,1)S(1)} %all_gather.18), kind=kOutput, calls=%fused_computation.22 | convolution fusion | flops 905969664 | bytes 15138816 | tf_op jit(solution)/shard_map/dot_general | solution.py:125
  242.7 1.5 scatter.50
  244.5 1.5 scatter.51
  246.9 4.6 fusion.12
  253.5 3.1 and_reduce_fusion.2
  256.6 17.3 %reduce-scatter.6.cloned.1.call-done = bf16[1,64,768]{2,1,0:T(8,128)(2,1)} async-done(((bf16[1,64,3072]{2,1,0:T(8,128)(2,1)}), bf16[1,64,768]{2,1,0:T(8,128)(2,1)}) %reduce-scatter.6.cloned.1.call-update) | async-done | bytes 98320 | tf_op jit(solution)/shard_map/reduce_scatter | solution.py:139
  273.9 1.6 select_select_fusion
  277.9 8.6 %all-reduce.6 = (f32[1,64]{1,0:T(1,128)S(1)}, f32[1,64]{1,0:T(1,128)S(1)}) all-reduce(f32[1,64]{1,0:T(1,128)S(1)} %bitcast.438, f32[1,64]{1,0:T(1,128)S(1)} %bitcast.437), channel_id=1, replica_groups=mesh['section'=2,'row'=32,'col'=4] {'col'}, use_global_device_ids=true, to_apply=%region_13.14 | all-reduce | flops 128 | bytes 1024 | tf_op jit(solution)/shard_map/psum | solution.py:71
  286.7 12.9 %all_gather.20 = bf16[1,64,3072]{2,1,0:T(8,128)(2,1)S(1)} all-gather(bf16[1,64,768]{2,1,0:T(8,128)(2,1)S(1)} %fusion.62), channel_id=1, replica_groups=mesh['section'=2,'row'=32,'col'=4] {'col'}, dimensions={2}, use_global_device_ids=true | all-gather | bytes 491520 | tf_op jit(solution)/shard_map/all_gather | solution.py:82
  299.5 9.4 %fusion.20 = f32[1,64,3,768]{3,1,2,0:T(8,128)S(1)} fusion(bf16[1,3072,3,768]{1,3,2,0:T(8,128)(2,1)} %copy.139, bf16[1,64,3072]{2,1,0:T(8,128)(2,1)S(1)} %all_gather.20), kind=kOutput, calls=%fused_computation.23 | convolution fusion | flops 905969664 | bytes 15138816 | tf_op jit(solution)/shard_map/dot_general | solution.py:125
  315.3 4.6 fusion.13
  320.8 1.5 scatter.54
  322.3 21.0 %reduce-scatter.8.cloned.1.call-done = bf16[1,64,768]{2,1,0:T(8,128)(2,1)} async-done(((bf16[1,64,3072]{2,1,0:T(8,128)(2,1)}), bf16[1,64,768]{2,1,0:T(8,128)(2,1)}) %reduce-scatter.8.cloned.1.call-update) | async-done | bytes 98320 | tf_op jit(solution)/shard_map/reduce_scatter | solution.py:139
  343.3 2.2 fusion.151
  347.8 8.6 %all-reduce.5 = (f32[1,64]{1,0:T(1,128)S(1)}, f32[1,64]{1,0:T(1,128)S(1)}) all-reduce(f32[1,64]{1,0:T(1,128)S(1)} %bitcast.440, f32[1,64]{1,0:T(1,128)S(1)} %bitcast.439), channel_id=1, replica_groups=mesh['section'=2,'row'=32,'col'=4] {'col'}, use_global_device_ids=true, to_apply=%region_22.23 | all-reduce | flops 128 | bytes 1024 | tf_op jit(solution)/shard_map/psum | solution.py:71
  356.6 12.7 %all_gather.21 = bf16[1,64,3072]{2,1,0:T(8,128)(2,1)S(1)} all-gather(bf16[1,64,768]{2,1,0:T(8,128)(2,1)S(1)} %fusion.69), channel_id=1, replica_groups=mesh['section'=2,'row'=32,'col'=4] {'col'}, dimensions={2}, use_global_device_ids=true | all-gather | bytes 491520 | tf_op jit(solution)/shard_map/all_gather | solution.py:82
  369.2 9.4 %fusion.23 = f32[1,64,3,768]{3,1,2,0:T(8,128)S(1)} fusion(bf16[1,3072,3,768]{1,3,2,0:T(8,128)(2,1)} %copy.139, bf16[1,64,3072]{2,1,0:T(8,128)(2,1)S(1)} %all_gather.21), kind=kOutput, calls=%fused_computation.24 | convolution fusion | flops 905969664 | bytes 15138816 | tf_op jit(solution)/shard_map/dot_general | solution.py:125
  379.6 2.1 fusion.107
  381.8 1.5 scatter.61
  383.3 1.5 scatter.60
  386.1 4.6 fusion.14
  392.9 21.1 %reduce-scatter.10.cloned.1.call-done = bf16[1,64,768]{2,1,0:T(8,128)(2,1)} async-done(((bf16[1,64,3072]{2,1,0:T(8,128)(2,1)}), bf16[1,64,768]{2,1,0:T(8,128)(2,1)}) %reduce-scatter.10.cloned.1.call-update) | async-done | bytes 98320 | tf_op jit(solution)/shard_map/reduce_scatter | solution.py:139
  414.0 2.3 fusion.150
  416.4 1.5 collective-permute-start.2
  418.8 8.6 %all-reduce.4 = (f32[1,64]{1,0:T(1,128)S(1)}, f32[1,64]{1,0:T(1,128)S(1)}) all-reduce(f32[1,64]{1,0:T(1,128)S(1)} %bitcast.442, f32[1,64]{1,0:T(1,128)S(1)} %bitcast.441), channel_id=1, replica_groups=mesh['section'=2,'row'=32,'col'=4] {'col'}, use_global_device_ids=true, to_apply=%region_31.32 | all-reduce | flops 128 | bytes 1024 | tf_op jit(solution)/shard_map/psum | solution.py:71
  427.5 12.7 %all_gather.22 = bf16[1,64,3072]{2,1,0:T(8,128)(2,1)S(1)} all-gather(bf16[1,64,768]{2,1,0:T(8,128)(2,1)S(1)} %fusion.76), channel_id=1, replica_groups=mesh['section'=2,'row'=32,'col'=4] {'col'}, dimensions={2}, use_global_device_ids=true | all-gather | bytes 491520 | tf_op jit(solution)/shard_map/all_gather | solution.py:82
  440.2 9.4 %fusion.26 = f32[1,64,3,768]{3,1,2,0:T(8,128)S(1)} fusion(bf16[1,3072,3,768]{1,3,2,0:T(8,128)(2,1)} %copy.139, bf16[1,64,3072]{2,1,0:T(8,128)(2,1)S(1)} %all_gather.22), kind=kOutput, calls=%fused_computation.25 | convolution fusion | flops 905969664 | bytes 15138816 | tf_op jit(solution)/shard_map/dot_general | solution.py:125
  450.6 2.1 fusion.109
  456.9 4.6 fusion.15
  462.2 1.5 scatter.64
  463.7 21.0 %reduce-scatter.12.cloned.1.call-done = bf16[1,64,768]{2,1,0:T(8,128)(2,1)} async-done(((bf16[1,64,3072]{2,1,0:T(8,128)(2,1)}), bf16[1,64,768]{2,1,0:T(8,128)(2,1)}) %reduce-scatter.12.cloned.1.call-update) | async-done | bytes 98320 | tf_op jit(solution)/shard_map/reduce_scatter | solution.py:139
  484.8 2.3 fusion.149
  489.4 8.6 %all-reduce.3 = (f32[1,64]{1,0:T(1,128)S(1)}, f32[1,64]{1,0:T(1,128)S(1)}) all-reduce(f32[1,64]{1,0:T(1,128)S(1)} %bitcast.436, f32[1,64]{1,0:T(1,128)S(1)} %bitcast.435), channel_id=1, replica_groups=mesh['section'=2,'row'=32,'col'=4] {'col'}, use_global_device_ids=true, to_apply=%region_40.41 | all-reduce | flops 128 | bytes 1024 | tf_op jit(solution)/shard_map/psum | solution.py:71
  498.2 12.9 %all_gather.23 = bf16[1,64,3072]{2,1,0:T(8,128)(2,1)S(1)} all-gather(bf16[1,64,768]{2,1,0:T(8,128)(2,1)S(1)} %fusion.83), channel_id=1, replica_groups=mesh['section'=2,'row'=32,'col'=4] {'col'}, dimensions={2}, use_global_device_ids=true | all-gather | bytes 491520 | tf_op jit(solution)/shard_map/all_gather | solution.py:82
  511.1 9.4 %fusion.29 = f32[1,64,3,768]{3,1,2,0:T(8,128)S(1)} fusion(bf16[1,3072,3,768]{1,3,2,0:T(8,128)(2,1)} %copy.139, bf16[1,64,3072]{2,1,0:T(8,128)(2,1)S(1)} %all_gather.23), kind=kOutput, calls=%fused_computation.26 | convolution fusion | flops 905969664 | bytes 15138816 | tf_op jit(solution)/shard_map/dot_general | solution.py:125
  527.1 4.6 fusion.16
  531.8 1.5 scatter.69
  533.3 21.8 %reduce-scatter.14.cloned.1.call-done = bf16[1,64,768]{2,1,0:T(8,128)(2,1)} async-done(((bf16[1,64,3072]{2,1,0:T(8,128)(2,1)}), bf16[1,64,768]{2,1,0:T(8,128)(2,1)}) %reduce-scatter.14.cloned.1.call-update) | async-done | bytes 98320 | tf_op jit(solution)/shard_map/reduce_scatter | solution.py:139
  555.0 2.3 fusion.128
  (208 shorter events, 43.5 us)
Async XLA Ops:
  6.5 204.1 %all-gather.2.cloned.1.call-start = ((), (), s32[]{:S(2)}) async-start(), calls=%async_computation.6 | async-start | bytes 14598144 | tf_op jit(solution)/shard_map/all_gather | solution.py:92
  10.9 12.0 %copy-start.3 = (s32[1,4]{1,0:T(1,128)S(1)}, s32[1,4]{1,0:T(1,128)}, u32[]{:S(2)}) copy-start(s32[1,4]{1,0:T(1,128)} %param.39) | copy-start | bytes 52
  10.9 17.4 %copy-start.2 = (bf16[1,1,256,768]{3,2,1,0:T(8,128)(2,1)S(1)}, bf16[1,1,256,768]{3,2,1,0:T(8,128)(2,1)}, u32[]{:S(2)}) copy-start(bf16[1,1,256,768]{3,2,1,0:T(8,128)(2,1)} %param.44) | copy-start | bytes 1179652
  10.9 17.4 %copy-start.1 = (bf16[1,1,256,768]{3,2,1,0:T(8,128)(2,1)S(1)}, bf16[1,1,256,768]{3,2,1,0:T(8,128)(2,1)}, u32[]{:S(2)}) copy-start(bf16[1,1,256,768]{3,2,1,0:T(8,128)(2,1)} %param.45) | copy-start | bytes 1179652
  10.9 236.0 %all-to-all-start = ((bf16[32,1,768,96]{2,3,1,0:T(8,128)(2,1)}), bf16[32,1,768,96]{2,3,1,0:T(8,128)(2,1)}, u32[]{:S(2)}, u32[]{:S(2)}) async-start(bf16[32,1,768,96]{2,3,1,0:T(8,128)(2,1)} %stack.2), calls=%async_computation | async-start | bytes 9437184 | tf_op jit(solution)/shard_map/all_to_all | solution.py:94
  22.8 251.1 %reduce-scatter.6.cloned.1.call-start = ((), (), s32[]{:S(2)}) async-start(), calls=%async_computation.7 | async-start | bytes 491520 | tf_op jit(solution)/shard_map/reduce_scatter | solution.py:139
  28.4 6.7 %copy-start = (bf16[1,256,768]{2,1,0:T(8,128)(2,1)S(1)}, bf16[1,256,768]{2,1,0:T(8,128)(2,1)}, u32[]{:S(2)}) copy-start(bf16[1,256,768]{2,1,0:T(8,128)(2,1)} %param.38) | copy-start | bytes 1179652
  35.1 15.1 %copy-start.4 = (s32[1,2]{1,0:T(1,128)S(1)}, s32[1,2]{1,0:T(1,128)}, u32[]{:S(2)}) copy-start(s32[1,2]{1,0:T(1,128)} %constant.478.clone.1) | copy-start | bytes 28
  35.1 17.0 %copy-start.5 = (s32[3]{0:T(128)S(1)}, s32[3]{0:T(128)}, u32[]{:S(2)}) copy-start(s32[3]{0:T(128)} %constant.479.clone.1) | copy-start | bytes 40
  251.6 91.7 %reduce-scatter.8.cloned.1.call-start = ((), (), s32[]{:S(2)}) async-start(), calls=%async_computation.8 | async-start | bytes 491520 | tf_op jit(solution)/shard_map/reduce_scatter | solution.py:139
  275.6 2.2 collective-permute-start
  320.0 94.1 %reduce-scatter.10.cloned.1.call-start = ((), (), s32[]{:S(2)}) async-start(), calls=%async_computation.9 | async-start | bytes 491520 | tf_op jit(solution)/shard_map/reduce_scatter | solution.py:139
  345.4 2.2 collective-permute-start.1
  385.5 28.6 %copy-start.7 = (pred[64]{0:T(512)(128)(4,1)S(1)}, pred[64]{0:T(512)(128)(4,1)}, u32[]{:S(2)}) copy-start(pred[64]{0:T(512)(128)(4,1)} %broadcast_and_fusion.2) | copy-start | bytes 196
  390.7 94.0 %reduce-scatter.12.cloned.1.call-start = ((), (), s32[]{:S(2)}) async-start(), calls=%async_computation.10 | async-start | bytes 491520 | tf_op jit(solution)/shard_map/reduce_scatter | solution.py:139
  416.4 2.2 collective-permute-start.2
  456.2 28.5 %copy-start.6 = (pred[64]{0:T(512)(128)(4,1)S(1)}, pred[64]{0:T(512)(128)(4,1)}, u32[]{:S(2)}) copy-start(pred[64]{0:T(512)(128)(4,1)} %broadcast_and_fusion.1) | copy-start | bytes 196
  461.5 93.6 %reduce-scatter.14.cloned.1.call-start = ((), (), s32[]{:S(2)}) async-start(), calls=%async_computation.11 | async-start | bytes 491520 | tf_op jit(solution)/shard_map/reduce_scatter | solution.py:139
  487.0 2.2 collective-permute-start.3
Sparse Core Ops, SparseCore 0:
  9.9 200.6 all-gather.1
  251.7 22.2 reduce-scatter.5
  320.1 23.1 reduce-scatter.7
  390.8 23.1 reduce-scatter.9
  461.6 23.0 reduce-scatter.11
  531.9 23.1 reduce-scatter.13
